TPU v7x, 128 devices: a whole 4x4x4 slice. The times are simulated.
128 devices in a mesh: cfg: 2 (over z_lo), seq: 8 (over x, core), blk: 8 (over z_hi, y).
Axes of the slice: x: 4, y: 4, z: 4 (z_hi: 2, z_lo: 2; z = z_hi * 2 + z_lo), core: 2. Of those that a mesh axis runs over, the one named last changes fastest.
Arguments:
- hidden: bfloat16 [2, 3072, 5120], P('cfg', 'seq', 'blk'), may hold values from -2.5 to 2.5
- modulation: float32 [3, 5120], replicated, may hold values from -4 to 4
- in_projection: bfloat16 [5120, 3, 3072], P(('cfg', 'seq'), None, 'blk'), may hold values from -0.078125 to 0.078125
- out_projection: bfloat16 [3072, 5120], P('blk', ('cfg', 'seq')), may hold values from -0.15625 to 0.15625
- lengths: int32 [5], replicated, may hold values from 1 to 1536, 3072 in all
- positions: int32 [3, 3072], P(None, 'seq'), may hold values from 0 to 63
- guidance: float32 [1], replicated, may hold values from 2 to 5
Outputs:
- guided: float32 [8, 2, 192, 5120], P('seq', 'cfg', None, 'blk')
Inputs may be any that keep to these rules, and one draw needn't show every extreme that they name: The clip lengths sum to 3072 and the longest is exactly 1536.
All inputs are finite; a program needn't handle non-finite values.
Results may differ from a plain program's by a relative error of at most 0.012.
The roundings to bfloat16 on the way count: a program that leaves them out, or rounds other values in their place, can miss the bound.
Values may be sent and summed in bfloat16 or wider, within the bound.
A program may use at most 128 MiB of HBM per device.

v0:
```python
import jax
import jax.numpy as jnp
import numpy as np
from jax import lax
from jax.sharding import PartitionSpec as P

HEAD_DIM = 128


def from_partner(array, axis, distance):
    return lax.ppermute(array, axis, [(i, i ^ 1 << distance) for i in range(lax.axis_size(axis))])


def rotary_angles(head_width):
    third = head_width // 6
    first_dim = head_width - 4 * third
    other_dim = 2 * third
    pair_index = np.arange(head_width) // 2
    first_pairs = first_dim // 2
    other_pairs = other_dim // 2
    in_first = pair_index < first_pairs
    in_second = (pair_index >= first_pairs) & (pair_index < first_pairs + other_pairs)
    in_third = pair_index >= first_pairs + other_pairs
    row_first = np.where(in_first, 10000.0 ** (-2.0 * pair_index / first_dim), 0.0)
    row_second = np.where(
        in_second, 10000.0 ** (-2.0 * (pair_index - first_pairs) / other_dim), 0.0
    )
    row_third = np.where(
        in_third, 10000.0 ** (-2.0 * (pair_index - first_pairs - other_pairs) / other_dim), 0.0
    )
    return np.stack([row_first, row_second, row_third]).astype(np.float32)


def turn_matrix(head_width):
    row_index = np.arange(head_width)[:, None]
    col_index = np.arange(head_width)[None, :]
    upper = np.where((col_index == row_index + 1) & (row_index % 2 == 0), 1.0, 0.0)
    lower = np.where((col_index == row_index - 1) & (row_index % 2 == 1), -1.0, 0.0)
    return (upper + lower).astype(np.float32)


def layer_norm(inputs):
    row_mean = jnp.mean(inputs, -1, keepdims=True)
    centered = inputs - row_mean
    variance = jnp.mean(centered * centered, -1, keepdims=True)
    return centered * lax.rsqrt(variance + 1e-06)


def rms_norm(inputs):
    return inputs * lax.rsqrt(jnp.mean(inputs * inputs, -1, keepdims=True) + 1e-06)


def rotate(inputs, cosine, sine, turning):
    turned = jnp.einsum("thd,de->the", inputs, turning, precision=lax.Precision.HIGHEST)
    return inputs * cosine + turned * sine


def clip_index(clip_ends, first_row, count):
    token_index = first_row + jnp.arange(count, dtype=jnp.int32)
    return jnp.sum((token_index[:, None] >= clip_ends[None, :]).astype(jnp.int32), 1)


def local(hidden, modulation, in_projection, out_projection, lengths, positions, guidance):
    states = hidden[0]
    tok_count = states.shape[0]
    feat_width = states.shape[1]
    half_rows = tok_count // 2
    inner_width = in_projection.shape[2]
    head_count = inner_width // HEAD_DIM
    full_states = lax.all_gather(states, "blk", axis=1, tiled=True)
    modulated = (
        layer_norm(full_states.astype(jnp.float32)) * (1.0 + modulation[1]) + modulation[0]
    ).astype(jnp.bfloat16)
    piece = lax.all_gather(in_projection, ("cfg", "seq"), axis=0, tiled=True)
    mixed = jnp.dot(
        modulated,
        piece.reshape(piece.shape[0], 3 * inner_width),
        preferred_element_type=jnp.float32,
    )
    mixed = mixed.reshape(tok_count, 3, head_count, HEAD_DIM)
    angle_table = jnp.asarray(rotary_angles(HEAD_DIM))
    turning = jnp.asarray(turn_matrix(HEAD_DIM))
    angles = jnp.einsum(
        "at,ae->te", positions.astype(jnp.float32), angle_table, precision=lax.Precision.HIGHEST
    )
    cosine = jnp.cos(angles)[:, None, :]
    sine = jnp.sin(angles)[:, None, :]
    queries = rotate(rms_norm(mixed[:, 0]), cosine, sine, turning).astype(jnp.bfloat16)
    key_rows = rotate(rms_norm(mixed[:, 1]), cosine, sine, turning).astype(jnp.bfloat16)
    value_rows = mixed[:, 2].astype(jnp.bfloat16)
    clip_ends = jnp.cumsum(lengths)
    query_clip = clip_index(clip_ends, lax.axis_index("seq") * tok_count, tok_count)
    score_scale = HEAD_DIM ** (-0.5)
    start_state = (
        jnp.zeros((tok_count, head_count, HEAD_DIM), jnp.float32),
        jnp.zeros((head_count, tok_count), jnp.float32),
    )
    first_row = jnp.int32(0)
    key_piece = lax.all_gather(key_rows, "seq", axis=0, tiled=True)
    value_piece = lax.all_gather(value_rows, "seq", axis=0, tiled=True)
    row_count = key_piece.shape[0]
    key_block = 512 if row_count % 512 == 0 else row_count

    def key_step(block_index, running):
        numerator, denominator = running
        key_slab = lax.dynamic_slice_in_dim(key_piece, block_index * key_block, key_block, 0)
        value_slab = lax.dynamic_slice_in_dim(value_piece, block_index * key_block, key_block, 0)
        key_clip = clip_index(clip_ends, first_row + block_index * key_block, key_block)
        scores = (
            jnp.einsum("qhd,khd->hqk", queries, key_slab, preferred_element_type=jnp.float32)
            * score_scale
        )
        same_clip = query_clip[:, None] == key_clip[None, :]
        weights = jnp.where(same_clip[None], jnp.exp(scores), 0.0)
        numerator = numerator + jnp.einsum(
            "hqk,khd->qhd",
            weights.astype(jnp.bfloat16),
            value_slab,
            preferred_element_type=jnp.float32,
        )
        denominator = denominator + jnp.sum(weights, -1)
        return (numerator, denominator)

    numerator, denominator = lax.fori_loop(0, row_count // key_block, key_step, start_state)
    attended = (
        (numerator / jnp.transpose(denominator)[:, :, None])
        .astype(jnp.bfloat16)
        .reshape(tok_count, inner_width)
    )
    col_start = lax.axis_index("blk") * feat_width
    own_inputs = states.astype(jnp.float32)
    cfg_index = lax.axis_index("cfg")
    partial_out = jnp.dot(
        attended,
        lax.all_gather(out_projection, ("cfg", "seq"), axis=1, tiled=True),
        preferred_element_type=jnp.float32,
    )
    projected = lax.psum_scatter(partial_out, "blk", scatter_dimension=1, tiled=True)
    gate_vector = lax.dynamic_slice_in_dim(modulation[2], col_start, feat_width, 0)
    block_out = own_inputs + gate_vector * projected
    other_out = from_partner(block_out, "cfg", 0)
    mine_rows = lax.dynamic_slice_in_dim(block_out, cfg_index * half_rows, half_rows, 0)
    their_rows = lax.dynamic_slice_in_dim(other_out, cfg_index * half_rows, half_rows, 0)
    is_cond = cfg_index == 0
    cond_rows = jnp.where(is_cond, mine_rows, their_rows)
    uncond_rows = jnp.where(is_cond, their_rows, mine_rows)
    guided = uncond_rows + guidance[0] * (cond_rows - uncond_rows)
    return guided.reshape(1, 1, half_rows, feat_width)


def solution(mesh):
    return jax.shard_map(
        local,
        mesh=mesh,
        in_specs=(
            P("cfg", "seq", "blk"),
            P(),
            P(("cfg", "seq"), None, "blk"),
            P("blk", ("cfg", "seq")),
            P(),
            P(None, "seq"),
            P(),
        ),
        out_specs=P("seq", "cfg", None, "blk"),
        check_vma=False,
    )
```

profile of v0, /device:TPU:0, one launch (start us, length us, event | category | flops | bytes accessed | tf_op | source)
XLA Modules:
  0.0 421.1 jit_solution(1140254993012736413)
XLA Ops:
  6.5 0.0 all-gather.14.cloned.1.call-start
  6.5 0.7 all-gather.14.cloned.1.call-update
  7.3 0.0 all-gather.8.cloned.1.call-start
  7.3 0.7 all-gather.8.cloned.1.call-update
  8.0 0.0 all-gather.16.cloned.1.call-start
  8.1 1.1 fusion.38
  9.2 72.2 %all-gather.14.cloned.1.call-done = bf16[1,384,5120]{2,1,0:T(8,128)(2,1)} async-done(((bf16[1,384,640]{2,1,0:T(8,128)(2,1)}), bf16[1,384,5120]{2,1,0:T(8,128)(2,1)}) %all-gather.14.cloned.1.call-update) | async-done | bytes 3932176 | tf_op jit(solution)/shard_map/all_gather | solution.py:70
  81.3 2.9 convert_reduce_fusion.1
  84.2 0.4 copy-done
  84.6 1.2 fusion.17
  85.8 63.0 %all-gather.8.cloned.1.call-done = bf16[5120,3,384]{2,0,1:T(8,128)(2,1)} async-done(((bf16[320,3,384]{2,0,1:T(8,128)(2,1)}), bf16[5120,3,384]{2,0,1:T(8,128)(2,1)}) %all-gather.8.cloned.1.call-update) | async-done | bytes 11796496 | tf_op jit(solution)/shard_map/all_gather | solution.py:74
  148.8 16.2 %copy.34 = bf16[5120,3,384]{0,2,1:T(8,128)(2,1)} copy(bf16[5120,3,384]{2,0,1:T(8,128)(2,1)} %all-gather.8.cloned.1.call-done) | data formatting | bytes 23592960 | tf_op jit(solution)/shard_map/all_gather | solution.py:74
  165.1 10.7 %fusion.22 = f32[384,3,3,128]{0,3,2,1:T(8,128)S(1)} fusion(bf16[3,3,128,5120]{3,2,1,0:T(8,128)(2,1)} %bitcast.94, bf16[1,384,5120]{2,1,0:T(8,128)(2,1)} %all-gather.14.cloned.1.call-done, f32[5120]{0:T(1024)S(1)} %bitcast.98, f32[5120]{0:T(1024)S(1)} %bitcast.99, f32[384]{0:T(512)S(1)} %add_rsqrt_fusion.2, f32[384]{0:T(512)S(1)} %broadcast_multiply_fusion), kind=kOutput, calls=%fused_computation.29 | convolution fusion | flops 4541644800 | bytes 17542144 | tf_op jit(solution)/shard_map/dot_general | solution.py:75
  175.7 0.0 copy-start.5
  175.7 0.7 slice.48
  176.5 0.0 all-gather.16.cloned.1.call-update
  176.5 0.0 all-gather.10.cloned.1.call-start
  176.6 1.1 cosine_bitcast_fusion
  177.7 0.1 multiply_reduce_fusion
  177.8 1.4 fusion.30
  179.2 0.0 all-gather.10.cloned.1.call-update
  179.2 0.0 all-gather.12.cloned.1.call-start
  179.3 0.5 all-gather.12.cloned.1.call-update
  179.8 0.2 reduce-scatter.2.cloned.1.call-start
  180.1 0.2 reduce-window.8
  180.3 0.1 convert_reduce_fusion.2
  180.3 0.7 fusion.31
  181.0 0.2 copy.40
  181.3 22.3 %all-gather.16.cloned.1.call-done = bf16[3072,1,3,128]{0,3,2,1:T(8,128)(2,1)} async-done(((bf16[384,1,3,128]{0,3,2,1:T(8,128)(2,1)}), bf16[3072,1,3,128]{0,3,2,1:T(8,128)(2,1)}) %all-gather.16.cloned.1.call-update) | async-done | bytes 2359312 | tf_op jit(solution)/shard_map/all_gather | solution.py:100
  203.6 27.7 %all-gather.10.cloned.1.call-done = bf16[3072,3,128]{0,2,1:T(8,128)(2,1)} async-done(((bf16[384,3,128]{0,2,1:T(8,128)(2,1)}), bf16[3072,3,128]{0,2,1:T(8,128)(2,1)}) %all-gather.10.cloned.1.call-update) | async-done | bytes 2359312 | tf_op jit(solution)/shard_map/all_gather | solution.py:99
  231.3 22.9 %while.16 = (s32[]{:T(128)}, f32[384,3,128]{0,2,1:T(8,128)S(1)}, f32[3,384]{1,0:T(4,128)S(1)}, bf16[3072,3,128]{0,2,1:T(8,128)(2,1)}, s32[384]{0:T(512)S(1)}, /*...) while((s32[]{:T(128)}, f32[384,3,128]{0,2,1:T(8,128)S(1)}, ...), condition=%wide.region_9.10_spmd.clone, body=%wide.region_6.9_spmd.clone.sunk | while | flops 306029184 | bytes 7597782 | solution.py:124
  231.3 0.1 convert_reduce_fusion.4
  231.4 0.2 broadcast_compare_fusion.2
  231.6 1.8 fusion.57
  233.4 1.7 fusion.58
  235.1 0.1 convert_reduce_fusion.4
  235.2 0.2 broadcast_compare_fusion.2
  235.4 1.8 fusion.57
  237.2 1.7 fusion.58
  238.9 0.1 convert_reduce_fusion.4
  239.0 0.2 broadcast_compare_fusion.2
  239.2 1.8 fusion.57
  241.0 1.7 fusion.58
  242.7 0.1 convert_reduce_fusion.4
  242.8 0.2 broadcast_compare_fusion.2
  243.0 1.8 fusion.57
  244.8 1.7 fusion.58
  246.6 0.1 convert_reduce_fusion.4
  246.6 0.2 broadcast_compare_fusion.2
  246.8 1.9 fusion.57
  248.7 1.7 fusion.58
  250.4 0.1 convert_reduce_fusion.4
  250.5 0.2 broadcast_compare_fusion.2
  250.6 1.9 fusion.57
  252.5 1.7 fusion.58
  254.2 0.1 divide_convert_fusion
  254.3 15.6 %all-gather.12.cloned.1.call-done = bf16[384,5120]{0,1:T(8,128)(2,1)} async-done(((bf16[384,320]{0,1:T(8,128)(2,1)}), bf16[384,5120]{0,1:T(8,128)(2,1)}) %all-gather.12.cloned.1.call-update) | async-done | bytes 3932176 | tf_op jit(solution)/shard_map/all_gather | solution.py:135
  269.9 7.4 %fusion.41 = f32[384,5120]{1,0:T(8,128)} fusion(bf16[384,384]{0,1:T(8,128)(2,1)S(1)} %bitcast.96, bf16[384,5120]{0,1:T(8,128)(2,1)} %all-gather.12.cloned.1.call-done), kind=kOutput, calls=%fused_computation.65 | convolution fusion | flops 1509949440 | bytes 12091392 | tf_op jit(solution)/shard_map/dot_general | solution.py:133
  277.3 0.0 reduce-scatter.2.cloned.1.call-update
  277.4 111.9 %reduce-scatter.2.cloned.1.call-done = f32[384,640]{1,0:T(8,128)} async-done(((f32[384,5120]{1,0:T(8,128)}), f32[384,640]{1,0:T(8,128)}) %reduce-scatter.2.cloned.1.call-update) | async-done | bytes 983056 | tf_op jit(solution)/shard_map/reduce_scatter | solution.py:138
  389.3 1.3 convert_add_fusion
  390.6 0.7 collective-permute-start
  392.0 21.4 %collective-permute-done = f32[384,640]{1,0:T(8,128)S(1)} collective-permute-done((f32[384,640]{1,0:T(8,128)S(1)}, f32[384,640]{1,0:T(8,128)S(1)}, u32[]{:S(2)}, u32[]{:S(2)}) %collective-permute-start) | collective-permute-done | bytes 983072 | tf_op jit(solution)/shard_map/ppermute | solution.py:11
  413.3 0.9 add_bitcast_fusion
  (30 shorter events, 0.2 us)
Async XLA Ops:
  6.5 74.8 %all-gather.14.cloned.1.call-start = ((), (), s32[]{:S(2)}) async-start(), calls=%async_computation.5 | async-start | bytes 4423680 | tf_op jit(solution)/shard_map/all_gather | solution.py:70
  7.3 141.6 %all-gather.8.cloned.1.call-start = ((), (), s32[]{:S(2)}) async-start(), calls=%async_computation.1 | async-start | bytes 12533760 | tf_op jit(solution)/shard_map/all_gather | solution.py:74
  8.0 195.6 %all-gather.16.cloned.1.call-start = ((), (), s32[]{:S(2)}) async-start(), calls=%async_computation.6 | async-start | bytes 2654208 | tf_op jit(solution)/shard_map/all_gather | solution.py:100
  81.3 3.3 copy-start
  165.0 11.5 %copy-start.3 = (s32[3,384]{1,0:T(4,128)S(1)}, s32[3,384]{1,0:T(4,128)}, u32[]{:S(2)}) copy-start(s32[3,384]{1,0:T(4,128)} %param.16) | copy-start | bytes 13828
  165.0 11.5 %copy-start.4 = (f32[3,128]{1,0:T(4,128)S(1)}, f32[3,128]{1,0:T(4,128)}, u32[]{:S(2)}) copy-start(f32[3,128]{1,0:T(4,128)} %constant.88.clone) | copy-start | bytes 4612
  165.1 12.7 %copy-start.2 = (f32[128,128,1]{1,0,2:T(8,128)S(1)}, f32[128,128,1]{1,0,2:T(8,128)}, u32[]{:S(2)}) copy-start(f32[128,128,1]{1,0,2:T(8,128)} %constant.91) | copy-start | bytes 196612
  175.7 4.3 %copy-start.5 = (s32[5]{0:T(128)S(1)}, s32[5]{0:T(128)}, u32[]{:S(2)}) copy-start(s32[5]{0:T(128)} %param.15) | copy-start | bytes 64
  176.5 54.8 %all-gather.10.cloned.1.call-start = ((), (), s32[]{:S(2)}) async-start(), calls=%async_computation.2 | async-start | bytes 2654208 | tf_op jit(solution)/shard_map/all_gather | solution.py:99
  179.2 90.7 %all-gather.12.cloned.1.call-start = ((), (), s32[]{:S(2)}) async-start(), calls=%async_computation.3 | async-start | bytes 4177920 | tf_op jit(solution)/shard_map/all_gather | solution.py:135
  179.8 209.5 %reduce-scatter.2.cloned.1.call-start = ((), (), s32[]{:S(2)}) async-start(), calls=%async_computation.4 | async-start | bytes 8847360 | tf_op jit(solution)/shard_map/reduce_scatter | solution.py:138
  277.3 112.0 %copy-start.1 = (bf16[1,384,640]{2,1,0:T(8,128)(2,1)S(1)}, bf16[1,384,640]{2,1,0:T(8,128)(2,1)}, u32[]{:S(2)}) copy-start(bf16[1,384,640]{2,1,0:T(8,128)(2,1)} %param.11) | copy-start | bytes 1474564
  390.6 22.8 %collective-permute-start = (f32[384,640]{1,0:T(8,128)S(1)}, f32[384,640]{1,0:T(8,128)S(1)}, u32[]{:S(2)}, u32[]{:S(2)}) collective-permute-start(f32[384,640]{1,0:T(8,128)S(1)} %convert_add_fusion), channel_id=1, source_target_pairs={{0,64},{64,0},{1,65},{65,1},{2,66},{66,2},{3,67},{67,3},{4,68},{68... | collective-permute-start | bytes 2949128 | tf_op jit(solution)/shard_map/ppermute | solution.py:11
Sparse Core Ops, SparseCore 0:
  9.7 71.6 all-gather.13
  83.0 65.7 all-gather.7
  176.6 26.8 all-gather.15
  205.1 26.1 all-gather.9
  232.8 36.9 all-gather.11
  277.5 111.7 reduce-scatter.1
where the time goes:
time: 422 us; the launch traced here: 421 us
  waiting for transfers between devices  336 us (80%)
  matrix products  42.3 us (10%)
  local copies, waits for them, and re-layouts  17.6 us (4%)
  between operations  14.2 us (3%)
  other arithmetic  9.41 us (2%)
    reduce_scatter x1, waiting for transfers between devices, local(): lax.psum_scatter(partial_out, 'blk', scatter_dimension=1, tiled=True)  112 us
    all_gather x1, waiting for transfers between devices, local(): full_states = lax.all_gather(states, 'blk', axis=1, tiled=True)  72.2 us
    all_gather x1, waiting for transfers between devices, local(): piece = lax.all_gather(in_projection, ('cfg', 'seq'), axis=0, tiled=True)  63 us
    all_gather x1, waiting for transfers between devices, local(): key_piece = lax.all_gather(key_rows, 'seq', axis=0, tiled=True)  27.7 us
    all_gather x1, waiting for transfers between devices, local(): value_piece = lax.all_gather(value_rows, 'seq', axis=0, tiled=True)  22.3 us
    ppermute x1, waiting for transfers between devices, from_partner(): lax.ppermute(array, axis, [(i, i ^ 1 << distance) for i in range(lax.axis...  21.4 us
    all_gather x1, local copies, waits for them, and re-layouts, local(): piece = lax.all_gather(in_projection, ('cfg', 'seq'), axis=0, tiled=True)  16.2 us
    all_gather x1, waiting for transfers between devices, local(): lax.all_gather(out_projection, ('cfg', 'seq'), axis=1, tiled=True)  15.6 us
  transfers between devices with their start and end apart: 7, of which 7 were waited for; matrix products, arithmetic and copies ran while one was open for 8% of the time, Pallas kernels for 0%

commit v1 on v0

--- a/solution.py
+++ b/solution.py
@@ -71,7 +71,12 @@
     modulated = (
         layer_norm(full_states.astype(jnp.float32)) * (1.0 + modulation[1]) + modulation[0]
     ).astype(jnp.bfloat16)
-    piece = lax.all_gather(in_projection, ("cfg", "seq"), axis=0, tiled=True)
+    piece = jnp.concatenate(
+        lax.all_to_all(
+            jnp.stack([in_projection] * lax.axis_size(("cfg", "seq"))), ("cfg", "seq"), 0, 0
+        ),
+        axis=0,
+    )
     mixed = jnp.dot(
         modulated,
         piece.reshape(piece.shape[0], 3 * inner_width),

time: 422 us -> 491 us (1.16)
  local copies, waits for them, and re-layouts: 17.6 us -> 49.8 us
  waiting for transfers between devices: 336 us -> 367 us
  starting transfers between devices: 1.11 us -> 7.19 us
    all_gather x1, waiting for transfers between devices: 72.2 us -> 168 us  [local(): full_states = lax.all_gather(states, 'blk', axis=1, tiled=True)]
    all_gather x1 -> x0, waiting for transfers between devices: 63 us -> none  [local(): piece = lax.all_gather(in_projection, ('cfg', 'seq'), axis=0, tiled=True)]
    another operation x0 -> x2, local copies, waits for them, and re-layouts: none -> 30.3 us  [the longest x1 22.9 us: local(): piece.reshape(piece.shape[0], 3 * inner_width)]
    all_to_all x0 -> x1, local copies, waits for them, and re-layouts: none -> 18.1 us  [local(): lax.all_to_all(jnp.stack([in_projection] * lax.axis_size(('cfg', 'seq')))...]
    all_gather x1 -> x0, local copies, waits for them, and re-layouts: 16.2 us -> none  [local(): piece = lax.all_gather(in_projection, ('cfg', 'seq'), axis=0, tiled=True)]
    all_to_all x0 -> x1, starting transfers between devices: none -> 6.05 us  [local(): lax.all_to_all(jnp.stack([in_projection] * lax.axis_size(('cfg', 'seq')))...]
  transfers between devices with their start and end apart: 7 -> 7, of which waited for: 7 -> 6; matrix products, arithmetic and copies ran while one was open for 8% -> 6% of each run, Pallas kernels for 0% -> 0%
where the time goes in v1:
time: 491 us; the launch traced here: 489 us
  waiting for transfers between devices  367 us (75%)
  local copies, waits for them, and re-layouts  49.8 us (10%)
  matrix products  42 us (9%)
  between operations  14 us (3%)
  other arithmetic  8.35 us (2%)
  starting transfers between devices  7.19 us (1%)
    all_gather x1, waiting for transfers between devices, local(): full_states = lax.all_gather(states, 'blk', axis=1, tiled=True)  168 us
    reduce_scatter x1, waiting for transfers between devices, local(): lax.psum_scatter(partial_out, 'blk', scatter_dimension=1, tiled=True)  112 us
    all_gather x1, waiting for transfers between devices, local(): key_piece = lax.all_gather(key_rows, 'seq', axis=0, tiled=True)  27.9 us
    another operation x1, local copies, waits for them, and re-layouts, local(): piece.reshape(piece.shape[0], 3 * inner_width)  22.9 us
    ppermute x1, waiting for transfers between devices, from_partner(): lax.ppermute(array, axis, [(i, i ^ 1 << distance) for i in range(lax.axis...  21.4 us
    all_gather x1, waiting for transfers between devices, local(): value_piece = lax.all_gather(value_rows, 'seq', axis=0, tiled=True)  21.3 us
    all_to_all x1, local copies, waits for them, and re-layouts, local(): lax.all_to_all(jnp.stack([in_projection] * lax.axis_size(('cfg', 'seq')))...  18.1 us
    all_gather x1, waiting for transfers between devices, local(): lax.all_gather(out_projection, ('cfg', 'seq'), axis=1, tiled=True)  15.6 us
  transfers between devices with their start and end apart: 7, of which 6 were waited for; matrix products, arithmetic and copies ran while one was open for 6% of the time, Pallas kernels for 0%

profile of v1, /device:TPU:0, one launch (start us, length us, event | category | flops | bytes accessed | tf_op | source)
XLA Modules:
  0.0 488.8 jit_solution(8324132556686049197)
XLA Ops:
  6.5 7.4 %stack.2 = bf16[16,320,3,384]{3,1,2,0:T(8,128)(2,1)} broadcast(bf16[320,3,384]{2,0,1:T(8,128)(2,1)} %param.13), dimensions={1,2,3} | broadcast | bytes 12533760 | tf_op jit(solution)/shard_map/stack | solution.py:76
  13.9 6.0 %all-to-all-start = ((bf16[16,320,3,384]{3,1,2,0:T(8,128)(2,1)}), bf16[16,320,3,384]{3,1,2,0:T(8,128)(2,1)}, u32[]{:S(2)}, u32[]{:S(2)}) async-start(bf16[16,320,3,384]{3,1,2,0:T(8,128)(2,1)} %stack.2), calls=%async_computation | async-start | bytes 23592960 | tf_op jit(solution)/shard_map/all_to_all | solution.py:75
  20.0 0.0 all-gather.11.cloned.1.call-start
  20.0 0.7 all-gather.11.cloned.1.call-update
  20.7 0.0 all-gather.13.cloned.1.call-start
  20.8 168.0 %all-gather.11.cloned.1.call-done = bf16[1,384,5120]{2,1,0:T(8,128)(2,1)} async-done(((bf16[1,384,640]{2,1,0:T(8,128)(2,1)}), bf16[1,384,5120]{2,1,0:T(8,128)(2,1)}) %all-gather.11.cloned.1.call-update) | async-done | bytes 3932176 | tf_op jit(solution)/shard_map/all_gather | solution.py:70
  188.8 2.9 convert_reduce_fusion.1
  191.7 0.4 copy-done
  192.1 1.2 fusion.17
  193.3 0.0 all-to-all-done
  193.3 18.1 %copy.35 = bf16[16,320,3,384]{1,0,3,2:T(8,128)(2,1)} copy(bf16[16,320,3,384]{3,1,2,0:T(8,128)(2,1)} %all-to-all-done) | data formatting | bytes 23592960 | tf_op jit(solution)/shard_map/all_to_all | solution.py:75
  211.4 22.9 %reshape_reshape.3 = bf16[5120,1152]{0,1:T(8,128)(2,1)} reshape(bf16[16,320,3,384]{1,0,3,2:T(8,128)(2,1)} %copy.35) | data formatting | bytes 23592960 | tf_op jit(solution)/shard_map/reshape;reshape | solution.py:82
  234.3 10.7 %fusion.22 = f32[384,3,3,128]{0,3,2,1:T(8,128)S(1)} fusion(bf16[3,3,128,5120]{3,2,1,0:T(8,128)(2,1)} %bitcast.96, bf16[1,384,5120]{2,1,0:T(8,128)(2,1)} %all-gather.11.cloned.1.call-done, f32[5120]{0:T(1024)S(1)} %bitcast.100, f32[5120]{0:T(1024)S(1)} %bitcast.101, f32[384]{0:T(512)S(1)} %add_rsqrt_fusion.2, f32[384]{0:T(512)S(1)} %broadcast_multiply_fusion), kind=kOutput, calls=%fused_computation.29 | convolution fusion | flops 4541644800 | bytes 17542144 | tf_op jit(solution)/shard_map/dot_general | solution.py:80
  244.9 0.0 copy-start.6
  244.9 0.7 slice.48
  245.7 0.0 all-gather.13.cloned.1.call-update
  245.7 0.0 all-gather.7.cloned.1.call-start
  245.8 1.1 cosine_bitcast_fusion
  246.9 0.1 multiply_reduce_fusion
  247.0 1.4 fusion.30
  248.4 0.0 all-gather.7.cloned.1.call-update
  248.4 0.0 all-gather.9.cloned.1.call-start
  248.5 0.5 all-gather.9.cloned.1.call-update
  249.0 0.2 reduce-scatter.2.cloned.1.call-start
  249.3 0.2 reduce-window.8
  249.5 0.1 convert_reduce_fusion.2
  249.5 0.7 fusion.31
  250.2 0.2 copy.41
  250.5 21.3 %all-gather.13.cloned.1.call-done = bf16[3072,1,3,128]{0,3,2,1:T(8,128)(2,1)} async-done(((bf16[384,1,3,128]{0,3,2,1:T(8,128)(2,1)}), bf16[3072,1,3,128]{0,3,2,1:T(8,128)(2,1)}) %all-gather.13.cloned.1.call-update) | async-done | bytes 2359312 | tf_op jit(solution)/shard_map/all_gather | solution.py:105
  271.8 27.9 %all-gather.7.cloned.1.call-done = bf16[3072,3,128]{0,2,1:T(8,128)(2,1)} async-done(((bf16[384,3,128]{0,2,1:T(8,128)(2,1)}), bf16[3072,3,128]{0,2,1:T(8,128)(2,1)}) %all-gather.7.cloned.1.call-update) | async-done | bytes 2359312 | tf_op jit(solution)/shard_map/all_gather | solution.py:104
  299.7 22.7 %while.16 = (s32[]{:T(128)}, f32[384,3,128]{0,2,1:T(8,128)S(1)}, f32[3,384]{1,0:T(4,128)S(1)}, bf16[3072,3,128]{0,2,1:T(8,128)(2,1)}, s32[384]{0:T(512)S(1)}, /*...) while((s32[]{:T(128)}, f32[384,3,128]{0,2,1:T(8,128)S(1)}, ...), condition=%wide.region_9.10_spmd.clone, body=%wide.region_6.9_spmd.clone.sunk | while | flops 306029184 | bytes 7597782 | solution.py:129
  299.7 0.1 convert_reduce_fusion.4
  299.8 0.2 broadcast_compare_fusion.2
  300.0 1.8 fusion.57
  301.8 1.6 fusion.58
  303.5 0.1 convert_reduce_fusion.4
  303.5 0.2 broadcast_compare_fusion.2
  303.7 1.8 fusion.57
  305.6 1.6 fusion.58
  307.2 0.1 convert_reduce_fusion.4
  307.3 0.2 broadcast_compare_fusion.2
  307.5 1.8 fusion.57
  309.3 1.6 fusion.58
  311.0 0.1 convert_reduce_fusion.4
  311.1 0.2 broadcast_compare_fusion.2
  311.3 1.8 fusion.57
  313.1 1.6 fusion.58
  314.8 0.1 convert_reduce_fusion.4
  314.9 0.2 broadcast_compare_fusion.2
  315.1 1.8 fusion.57
  316.9 1.6 fusion.58
  318.6 0.1 convert_reduce_fusion.4
  318.7 0.2 broadcast_compare_fusion.2
  318.9 1.8 fusion.57
  320.7 1.6 fusion.58
  322.4 0.1 divide_convert_fusion
  322.4 15.6 %all-gather.9.cloned.1.call-done = bf16[384,5120]{0,1:T(8,128)(2,1)} async-done(((bf16[384,320]{0,1:T(8,128)(2,1)}), bf16[384,5120]{0,1:T(8,128)(2,1)}) %all-gather.9.cloned.1.call-update) | async-done | bytes 3932176 | tf_op jit(solution)/shard_map/all_gather | solution.py:140
  338.1 7.4 %fusion.41 = f32[384,5120]{1,0:T(8,128)} fusion(bf16[384,384]{0,1:T(8,128)(2,1)S(1)} %bitcast.98, bf16[384,5120]{0,1:T(8,128)(2,1)} %all-gather.9.cloned.1.call-done), kind=kOutput, calls=%fused_computation.65 | convolution fusion | flops 1509949440 | bytes 12091392 | tf_op jit(solution)/shard_map/dot_general | solution.py:138
  345.5 0.0 reduce-scatter.2.cloned.1.call-update
  345.6 111.7 %reduce-scatter.2.cloned.1.call-done = f32[384,640]{1,0:T(8,128)} async-done(((f32[384,5120]{1,0:T(8,128)}), f32[384,640]{1,0:T(8,128)}) %reduce-scatter.2.cloned.1.call-update) | async-done | bytes 983056 | tf_op jit(solution)/shard_map/reduce_scatter | solution.py:143
  457.3 1.3 convert_add_fusion
  458.6 0.8 collective-permute-start
  460.0 21.4 %collective-permute-done = f32[384,640]{1,0:T(8,128)S(1)} collective-permute-done((f32[384,640]{1,0:T(8,128)S(1)}, f32[384,640]{1,0:T(8,128)S(1)}, u32[]{:S(2)}, u32[]{:S(2)}) %collective-permute-start) | collective-permute-done | bytes 983072 | tf_op jit(solution)/shard_map/ppermute | solution.py:11
  481.4 0.9 add_bitcast_fusion
  (33 shorter events, 0.2 us)
Async XLA Ops:
  13.9 6.8 %copy-start.3 = (f32[3,5120]{1,0:T(4,128)S(1)}, f32[3,5120]{1,0:T(4,128)}, u32[]{:S(2)}) copy-start(f32[3,5120]{1,0:T(4,128)} %param.12) | copy-start | bytes 184324
  13.9 179.3 %all-to-all-start = ((bf16[16,320,3,384]{3,1,2,0:T(8,128)(2,1)}), bf16[16,320,3,384]{3,1,2,0:T(8,128)(2,1)}, u32[]{:S(2)}, u32[]{:S(2)}) async-start(bf16[16,320,3,384]{3,1,2,0:T(8,128)(2,1)} %stack.2), calls=%async_computation | async-start | bytes 23592960 | tf_op jit(solution)/shard_map/all_to_all | solution.py:75
  20.0 168.8 %all-gather.11.cloned.1.call-start = ((), (), s32[]{:S(2)}) async-start(), calls=%async_computation.5 | async-start | bytes 4423680 | tf_op jit(solution)/shard_map/all_gather | solution.py:70
  20.7 251.1 %all-gather.13.cloned.1.call-start = ((), (), s32[]{:S(2)}) async-start(), calls=%async_computation.6 | async-start | bytes 2654208 | tf_op jit(solution)/shard_map/all_gather | solution.py:105
  188.8 3.3 copy-start
  234.2 11.5 %copy-start.4 = (s32[3,384]{1,0:T(4,128)S(1)}, s32[3,384]{1,0:T(4,128)}, u32[]{:S(2)}) copy-start(s32[3,384]{1,0:T(4,128)} %param.16) | copy-start | bytes 13828
  234.3 11.5 %copy-start.5 = (f32[3,128]{1,0:T(4,128)S(1)}, f32[3,128]{1,0:T(4,128)}, u32[]{:S(2)}) copy-start(f32[3,128]{1,0:T(4,128)} %constant.88.clone) | copy-start | bytes 4612
  234.3 12.7 %copy-start.2 = (f32[128,128,1]{1,0,2:T(8,128)S(1)}, f32[128,128,1]{1,0,2:T(8,128)}, u32[]{:S(2)}) copy-start(f32[128,128,1]{1,0,2:T(8,128)} %constant.91) | copy-start | bytes 196612
  244.9 4.3 copy-start.6
  245.7 54.0 %all-gather.7.cloned.1.call-start = ((), (), s32[]{:S(2)}) async-start(), calls=%async_computation.2 | async-start | bytes 2654208 | tf_op jit(solution)/shard_map/all_gather | solution.py:104
  248.4 89.7 %all-gather.9.cloned.1.call-start = ((), (), s32[]{:S(2)}) async-start(), calls=%async_computation.3 | async-start | bytes 4177920 | tf_op jit(solution)/shard_map/all_gather | solution.py:140
  249.0 208.3 %reduce-scatter.2.cloned.1.call-start = ((), (), s32[]{:S(2)}) async-start(), calls=%async_computation.4 | async-start | bytes 8847360 | tf_op jit(solution)/shard_map/reduce_scatter | solution.py:143
  345.5 111.8 %copy-start.1 = (bf16[1,384,640]{2,1,0:T(8,128)(2,1)S(1)}, bf16[1,384,640]{2,1,0:T(8,128)(2,1)}, u32[]{:S(2)}) copy-start(bf16[1,384,640]{2,1,0:T(8,128)(2,1)} %param.11) | copy-start | bytes 1474564
  458.6 22.8 %collective-permute-start = (f32[384,640]{1,0:T(8,128)S(1)}, f32[384,640]{1,0:T(8,128)S(1)}, u32[]{:S(2)}, u32[]{:S(2)}) collective-permute-start(f32[384,640]{1,0:T(8,128)S(1)} %convert_add_fusion), channel_id=1, source_target_pairs={{0,64},{64,0},{1,65},{65,1},{2,66},{66,2},{3,67},{67,3},{4,68},{68... | collective-permute-start | bytes 2949128 | tf_op jit(solution)/shard_map/ppermute | solution.py:11
Sparse Core Ops, SparseCore 0:
  23.1 165.6 all-gather.10
  245.8 25.9 all-gather.12
  273.5 26.1 all-gather.6
  301.2 36.7 all-gather.8
  345.7 111.5 reduce-scatter.1
